TPU v7x, 256 devices: a whole 4x4x8 slice. The times are simulated.
256 devices in a mesh: users: 64 (over x, z, y_hi), items: 4 (over y_lo, core).
Axes of the slice: x: 4, y: 4 (y_hi: 2, y_lo: 2; y = y_hi * 2 + y_lo), z: 8, core: 2. Of those that a mesh axis runs over, the one named last changes fastest.
Arguments:
- user_factors: bfloat16 [131072, 128], P('users'), may hold values from -0.5 to 0.5
- item_factors: float32 [4, 4, 512, 128], P('items', None, 'users'), may hold values from -6 to 6
- tile_user: int32 [64, 4, 4, 16], P('users', 'items'), may hold values from 0 to 7, as said below
- tile_item: int32 [64, 4, 4, 16], P('users', 'items'), may hold values from 0 to 1, as said below
- tile_count: int32 [64, 4, 4], P('users', 'items'), may hold values from 1 to 16, as said below
- ratings: bfloat16 [64, 4, 4, 16, 256, 256], P('users', 'items'), may hold values from -6 to 6
- mask: int32 [64, 4, 4, 16, 32, 256], P('users', 'items'), may hold values from 0 to 255
Outputs:
- new_items: float32 [4, 4, 512, 128], P('items', None, 'users')
- user_grad: float32 [131072, 128], P(('users', 'items'))
Inputs may be any that keep to these rules, and one draw needn't show every extreme that they name: `tile_user`: index of a user tile within its user block. `tile_item`: index of an item tile within its panel; the pairs (tile_user, tile_item) of one user block, owner and panel are distinct. Only the first tile_count slots of a user block, owner and panel hold observed tiles; the other slots are to be ignored. For every owner and panel some user block fills all 16 slots. Bit k of word mask[..., w, j] marks the rating in row 8 * w + k, column j of the tile as observed.
All inputs are finite; a program needn't handle non-finite values.
Results may differ from a plain program's by a relative error of at most 0.0031.
Values may be sent and summed in bfloat16 or wider, within the bound.
A program may use at most 128 MiB of HBM per device.

v0:
```python
import math
import jax
import jax.numpy as jnp
from jax import lax
from jax.sharding import PartitionSpec as P


def shards(user_factors, item_factors, tile_user, tile_item, tile_count, ratings, mask):
    users_count = lax.axis_size("users")
    rank_width = user_factors.shape[1]
    tile_side = ratings.shape[-1]
    user_tiles = user_factors.shape[0] // tile_side
    step_count = item_factors.shape[1]
    slot_count = ratings.shape[3]
    local_rows = item_factors.shape[2]
    panel_rows = local_rows * users_count
    panel_tiles = panel_rows // tile_side
    user_blocks = user_factors.reshape(user_tiles, tile_side, rank_width)
    step_rate = 8.0 / math.sqrt(tile_side * users_count)
    shifts = jnp.arange(8, dtype=jnp.int32)
    user_sum = jnp.zeros((user_tiles, tile_side, rank_width), jnp.float32)
    updated = []
    for step_index in range(step_count):
        panel_bf = lax.all_gather(
            item_factors[0, step_index].astype(jnp.bfloat16), "users", axis=0, tiled=True
        )
        tiles_of_panel = panel_bf.reshape(panel_tiles, tile_side, rank_width)
        user_index = tile_user[0, 0, step_index]
        item_index = tile_item[0, 0, step_index]
        user_rows = user_blocks[user_index]
        item_rows = tiles_of_panel[item_index]
        predicted = jnp.einsum(
            "tir,tjr->tij", user_rows, item_rows, preferred_element_type=jnp.float32
        )
        mask_bits = mask[0, 0, step_index][:, :, None, :] >> shifts[None, None, :, None] & 1
        observed = mask_bits.reshape(slot_count, tile_side, tile_side).astype(jnp.float32)
        live_slots = (jnp.arange(slot_count) < tile_count[0, 0, step_index]).astype(jnp.float32)
        errors = (
            observed
            * live_slots[:, None, None]
            * (predicted - ratings[0, 0, step_index].astype(jnp.float32))
        ).astype(jnp.bfloat16)
        tile_grad = jnp.einsum(
            "tij,tir->tjr", errors, user_rows, preferred_element_type=jnp.float32
        )
        item_onehot = (
            item_index[:, None] == jnp.arange(panel_tiles, dtype=jnp.int32)[None, :]
        ).astype(jnp.float32)
        panel_grad = jnp.einsum(
            "tp,tjr->pjr", item_onehot, tile_grad, precision=lax.Precision.HIGHEST
        ).reshape(panel_rows, rank_width)
        user_part = jnp.einsum(
            "tij,tjr->tir", errors, item_rows, preferred_element_type=jnp.float32
        )
        user_onehot = (
            user_index[:, None] == jnp.arange(user_tiles, dtype=jnp.int32)[None, :]
        ).astype(jnp.float32)
        user_sum = user_sum + jnp.einsum(
            "tu,tir->uir", user_onehot, user_part, precision=lax.Precision.HIGHEST
        )
        whole_sum = lax.psum(panel_grad, "users")
        own_rows = lax.dynamic_slice_in_dim(
            whole_sum, lax.axis_index("users") * local_rows, local_rows, 0
        )
        updated.append(0.95 * item_factors[0, step_index] - step_rate * own_rows)
    new_items = jnp.stack(updated)[None]
    user_terms = user_sum.reshape(user_tiles * tile_side, rank_width) / 32.0
    user_grad = lax.psum_scatter(user_terms, "items", scatter_dimension=0, tiled=True)
    return (new_items, user_grad)


def solution(mesh):
    return jax.shard_map(
        shards,
        mesh=mesh,
        in_specs=(
            P("users", None),
            P("items", None, "users", None),
            P("users", "items", None, None),
            P("users", "items", None, None),
            P("users", "items", None),
            P("users", "items", None, None, None, None),
            P("users", "items", None, None, None, None),
        ),
        out_specs=(P("items", None, "users", None), P(("users", "items"), None)),
        check_vma=False,
    )
```

profile of v0, /device:TPU:8, one launch (start us, length us, event | category | flops | bytes accessed | tf_op | source)
XLA Modules:
  0.0 1480.3 jit_solution(12672225782933500393)
XLA Ops:
  8.0 0.0 copy-start
  8.0 0.0 all-reduce.3.cloned.1.call-start
  8.1 1.5 fusion.89
  9.5 1.2 compare_convert_fusion.3
  10.7 1.2 compare_convert_fusion.2
  11.9 1.1 compare_convert_fusion
  13.0 1.3 compare_convert_fusion.1
  14.3 1.4 slice_bitcast_fusion.11
  15.7 0.8 fusion.76
  16.6 0.7 fusion.88
  17.4 0.7 shift_right_arithmetic.92
  18.0 184.3 %all-gather = bf16[1,1,512,128]{3,2,1,0:T(8,128)(2,1)S(1)} all-gather(bf16[1,1,8,128]{3,2,1,0:T(8,128)(2,1)S(1)} %get-tuple-element.14), channel_id=2, replica_groups=mesh['users'=64,'items'=4] {'users'}, dimensions={2}, use_global_device_ids=true | all-gather | bytes 133120 | tf_op jit(solution)/shard_map/all_gather | solution.py:24
  202.4 174.5 %all-gather.1 = bf16[1,1,512,128]{3,2,1,0:T(8,128)(2,1)S(1)} all-gather(bf16[1,1,8,128]{3,2,1,0:T(8,128)(2,1)S(1)} %get-tuple-element.15), channel_id=3, replica_groups=mesh['users'=64,'items'=4] {'users'}, dimensions={2}, use_global_device_ids=true | all-gather | bytes 133120 | tf_op jit(solution)/shard_map/all_gather | solution.py:24
  376.9 178.1 %all-gather.2 = bf16[1,1,512,128]{3,2,1,0:T(8,128)(2,1)S(1)} all-gather(bf16[1,1,8,128]{3,2,1,0:T(8,128)(2,1)S(1)} %get-tuple-element.16), channel_id=4, replica_groups=mesh['users'=64,'items'=4] {'users'}, dimensions={2}, use_global_device_ids=true | all-gather | bytes 133120 | tf_op jit(solution)/shard_map/all_gather | solution.py:24
  555.0 174.5 %all-gather.3 = bf16[1,1,512,128]{3,2,1,0:T(8,128)(2,1)S(1)} all-gather(bf16[1,1,8,128]{3,2,1,0:T(8,128)(2,1)S(1)} %get-tuple-element.17), channel_id=5, replica_groups=mesh['users'=64,'items'=4] {'users'}, dimensions={2}, use_global_device_ids=true | all-gather | bytes 133120 | tf_op jit(solution)/shard_map/all_gather | solution.py:24
  729.5 1.7 gather_fusion.4
  731.2 1.7 gather_fusion.6
  732.8 1.7 gather_fusion.2
  734.5 1.6 gather_fusion
  736.2 2.7 slice_bitcast_fusion.3
  738.9 1.6 gather_fusion.1
  740.5 3.5 fusion.7
  744.1 0.8 fusion.90
  744.9 2.0 fusion.34
  746.8 0.7 copy.9
  747.6 1.8 gather_fusion.3
  749.3 3.5 fusion.5
  752.9 0.0 copy-done.11
  752.9 0.0 copy-start.1
  752.9 0.8 fusion.91
  753.7 0.6 copy-done.1
  754.2 2.0 fusion.32
  756.2 0.7 copy.10
  757.0 1.7 gather_fusion.7
  758.7 3.5 fusion.1
  762.3 0.8 fusion.93
  763.0 0.5 copy-done.2
  763.5 2.1 fusion.28
  765.7 0.7 copy.12
  766.4 1.7 gather_fusion.5
  768.1 3.4 fusion.3
  771.6 0.8 fusion.92
  772.3 0.6 copy-done.4
  772.9 2.0 fusion.30
  774.9 0.7 copy.11
  775.6 0.0 all-reduce.3.cloned.1.call-update
  775.6 0.0 reduce-scatter.2.cloned.1.call-start
  775.7 2.7 fusion.95
  778.5 0.1 copy-done.8
  778.5 0.7 fusion.97
  779.2 0.9 copy-done.5
  780.1 0.3 copy-done.10
  780.4 0.7 fusion.96
  781.1 2.0 fusion.24
  783.1 2.0 fusion.20
  785.0 2.0 fusion.22
  787.0 0.7 fusion.94
  787.8 2.2 fusion.45
  790.0 0.0 copy-start.13
  790.0 1.2 copy.13
  791.1 0.0 reduce-scatter.2.cloned.1.call-update
  791.2 680.4 %all-reduce.3.cloned.1.call-done = (f32[512,128]{1,0:T(8,128)}, f32[512,128]{1,0:T(8,128)}, f32[512,128]{1,0:T(8,128)}, f32[512,128]{1,0:T(8,128)}) async-done(((f32[512,128]{1,0:T(8,128)}, f32[512,128]{1,0:T(8,128)}, f32[512,128]{1,0:T(8,128)}, f32[512,128]{1,0:T(8,128)}), (f32[512,128]{1,0:T(8,128)}, f32[512,128]{1,0:T(8,128)}, f32[512,128]{1,0:T(8,128)}, ...) | async-done | bytes 1048592 | tf_op jit(solution)/shard_map/psum | solution.py:61
  1471.5 0.7 fusion.51
  1472.3 0.6 maximum_bitcast_fusion
  (43 shorter events, 0.1 us)
Async XLA Ops:
  8.0 721.5 %copy-start = (bf16[2048,128]{1,0:T(8,128)(2,1)S(1)}, bf16[2048,128]{1,0:T(8,128)(2,1)}, u32[]{:S(2)}) copy-start(bf16[2048,128]{1,0:T(8,128)(2,1)} %param.7) | copy-start | bytes 1572868
  8.0 1463.5 %all-reduce.3.cloned.1.call-start = ((), (), s32[]{:S(2)}) async-start(), calls=%async_computation.2 | async-start | bytes 2097152 | tf_op jit(solution)/shard_map/psum | solution.py:61
  740.5 3.6 copy-start.12
  744.1 0.8 copy-start.17
  749.3 3.5 copy-start.11
  752.9 1.4 copy-start.1
  752.9 1.3 copy-start.16
  754.2 4.4 copy-start.18
  754.2 4.4 copy-start.20
  758.7 3.5 copy-start.9
  762.2 1.3 copy-start.2
  762.2 1.3 copy-start.15
  763.5 4.5 copy-start.19
  768.1 3.5 copy-start.7
  771.5 1.4 copy-start.4
  772.9 2.8 copy-start.14
  775.6 697.2 %reduce-scatter.2.cloned.1.call-start = ((), (), s32[]{:S(2)}) async-start(), calls=%async_computation.1 | async-start | bytes 1310720 | tf_op jit(solution)/shard_map/reduce_scatter | solution.py:68
  775.7 2.7 copy-start.3
  775.7 2.8 copy-start.8
  778.5 1.6 copy-start.5
  778.5 1.9 copy-start.10
  785.0 2.0 copy-start.6
  790.0 681.6 %copy-start.13 = (f32[1,4,8,128]{3,2,1,0:T(8,128)S(1)}, f32[1,4,8,128]{3,2,1,0:T(8,128)}, u32[]{:S(2)}) copy-start(f32[1,4,8,128]{3,2,1,0:T(8,128)} %param.8) | copy-start | bytes 49156
Sparse Core Ops, SparseCore 0:
  775.8 695.7 all-reduce.2
Sparse Core Ops, SparseCore 1:
  791.3 17.1 reduce-scatter.1
where the time goes:
time: 1480 us
  blocking collectives  711 us (48%)
  waiting for transfers between devices  680 us (46%)
  matrix products  38.1 us (3%)
  local copies, waits for them, and re-layouts  27.5 us (2%)
  between operations  15.9 us (1%)
    all_gather x4, blocking collectives, shards(): lax.all_gather(item_factors[0, step_index].astype(jnp.bfloat16), 'users',...  711 us
    psum x1, waiting for transfers between devices, shards(): whole_sum = lax.psum(panel_grad, 'users')  680 us
  transfers between devices with their start and end apart: 2, of which 1 were waited for; matrix products, arithmetic and copies ran while one was open for 1% of the time, Pallas kernels for 0%

commit v1 on v0

--- a/solution.py
+++ b/solution.py
@@ -21,8 +21,16 @@
     user_sum = jnp.zeros((user_tiles, tile_side, rank_width), jnp.float32)
     updated = []
     for step_index in range(step_count):
-        panel_bf = lax.all_gather(
-            item_factors[0, step_index].astype(jnp.bfloat16), "users", axis=0, tiled=True
+        panel_bf = jnp.concatenate(
+            lax.all_to_all(
+                jnp.stack(
+                    [item_factors[0, step_index].astype(jnp.bfloat16)] * lax.axis_size("users")
+                ),
+                "users",
+                0,
+                0,
+            ),
+            axis=0,
         )
         tiles_of_panel = panel_bf.reshape(panel_tiles, tile_side, rank_width)
         user_index = tile_user[0, 0, step_index]

time: 1480 us -> 838 us (0.57)
  blocking collectives: 711 us -> 0 us
  starting transfers between devices: 0.08 us -> 43.6 us
  waiting for transfers between devices: 680 us -> 703 us
    all_gather x4 -> x0, blocking collectives: 711 us -> none  [shards(): lax.all_gather(item_factors[0, step_index].astype(jnp.bfloat16), 'users',...]
    all_to_all x0 -> x4, starting transfers between devices: none -> 43.4 us  [shards(): lax.all_to_all(jnp.stack([item_factors[0, step_index].astype(jnp.bfloat16...]
  transfers between devices with their start and end apart: 2 -> 6, of which waited for: 1 -> 4; matrix products, arithmetic and copies ran while one was open for 1% -> 6% of each run, Pallas kernels for 0% -> 0%
where the time goes in v1:
time: 838 us; the launch traced here: 837 us
  waiting for transfers between devices  703 us (84%)
  starting transfers between devices  43.6 us (5%)
  matrix products  43.2 us (5%)
  local copies, waits for them, and re-layouts  26.4 us (3%)
  between operations  15.9 us (2%)
    psum x1, waiting for transfers between devices, shards(): whole_sum = lax.psum(panel_grad, 'users')  692 us
    all_to_all x4, starting transfers between devices, shards(): lax.all_to_all(jnp.stack([item_factors[0, step_index].astype(jnp.bfloat16...  43.4 us
  transfers between devices with their start and end apart: 6, of which 4 were waited for; matrix products, arithmetic and copies ran while one was open for 6% of the time, Pallas kernels for 0%

profile of v1, /device:TPU:8, one launch (start us, length us, event | category | flops | bytes accessed | tf_op | source)
XLA Modules:
  0.0 837.0 jit_solution(11438922863057177773)
XLA Ops:
  8.0 0.8 fusion.60
  8.8 0.7 stack.20
  9.5 13.7 %all-to-all-start.1 = ((bf16[64,8,128]{2,1,0:T(8,128)(2,1)}), bf16[64,8,128]{2,1,0:T(8,128)(2,1)S(1)}, u32[]{:S(2)}, u32[]{:S(2)}) async-start(bf16[64,8,128]{2,1,0:T(8,128)(2,1)} %stack.20), calls=%async_computation.1 | async-start | bytes 262144 | tf_op jit(solution)/shard_map/all_to_all | solution.py:25
  23.2 0.8 slice_bitcast_fusion.10
  24.0 0.8 slice_bitcast_fusion.11
  24.8 0.8 fusion.80
  25.7 1.5 fusion.92
  27.1 0.6 compare_convert_fusion.3
  27.8 0.6 compare_convert_fusion.2
  28.4 0.7 compare_convert_fusion
  29.0 0.7 compare_convert_fusion.1
  29.8 0.1 shift_right_arithmetic.92
  29.9 1.6 gather_fusion.4
  31.6 1.7 gather_fusion.6
  33.3 0.7 gather_fusion.2
  34.1 1.8 gather_fusion
  35.8 2.8 slice_bitcast_fusion.3
  38.6 0.7 stack.24
  39.3 12.7 %all-to-all-start.3 = ((bf16[64,8,128]{2,1,0:T(8,128)(2,1)}), bf16[64,8,128]{2,1,0:T(8,128)(2,1)S(1)}, u32[]{:S(2)}, u32[]{:S(2)}) async-start(bf16[64,8,128]{2,1,0:T(8,128)(2,1)} %stack.24), calls=%async_computation.3 | async-start | bytes 262144 | tf_op jit(solution)/shard_map/all_to_all | solution.py:25
  52.0 0.7 gather_fusion.3
  52.8 2.8 fusion.5
  55.6 2.0 fusion.98
  57.6 0.8 fusion.94
  58.4 5.8 all-to-all-done.3
  64.2 0.7 stack.22
  64.9 7.0 all-to-all-start.2
  71.8 1.7 gather_fusion.7
  73.5 3.5 fusion.1
  77.1 2.0 fusion.100
  79.1 2.1 fusion.96
  81.3 2.7 all-to-all-done.2
  84.0 0.7 stack.18
  84.7 10.0 %all-to-all-start = ((bf16[64,8,128]{2,1,0:T(8,128)(2,1)}), bf16[64,8,128]{2,1,0:T(8,128)(2,1)S(1)}, u32[]{:S(2)}, u32[]{:S(2)}) async-start(bf16[64,8,128]{2,1,0:T(8,128)(2,1)} %stack.18), calls=%async_computation | async-start | bytes 262144 | tf_op jit(solution)/shard_map/all_to_all | solution.py:25
  94.7 0.2 all-reduce.3.cloned.1.call-start
  94.9 1.7 gather_fusion.5
  96.6 3.5 fusion.3
  100.2 2.1 fusion.99
  102.3 2.1 fusion.95
  104.4 2.5 all-to-all-done
  106.9 1.7 gather_fusion.1
  108.6 3.4 fusion.7
  112.1 0.8 fusion.93
  112.8 0.6 copy-done.6
  113.4 2.0 fusion.34
  115.4 0.7 copy.9
  116.1 2.0 fusion.32
  118.1 0.7 copy.10
  118.8 2.0 fusion.28
  120.8 0.7 copy.12
  121.6 2.2 fusion.30
  123.8 0.7 copy.11
  124.5 3.0 fusion.24
  127.5 0.0 all-reduce.3.cloned.1.call-update
  127.5 0.0 reduce-scatter.2.cloned.1.call-start
  127.6 2.0 fusion.20
  129.6 2.0 fusion.22
  131.6 0.7 fusion.97
  132.3 0.5 copy-done.16
  132.9 2.2 fusion.45
  135.1 1.2 copy.13
  136.2 0.0 reduce-scatter.2.cloned.1.call-update
  136.3 691.9 %all-reduce.3.cloned.1.call-done = (f32[512,128]{1,0:T(8,128)}, f32[512,128]{1,0:T(8,128)}, f32[512,128]{1,0:T(8,128)}, f32[512,128]{1,0:T(8,128)}) async-done(((f32[512,128]{1,0:T(8,128)}, f32[512,128]{1,0:T(8,128)}, f32[512,128]{1,0:T(8,128)}, f32[512,128]{1,0:T(8,128)}), (f32[512,128]{1,0:T(8,128)}, f32[512,128]{1,0:T(8,128)}, f32[512,128]{1,0:T(8,128)}, ...) | async-done | bytes 1048592 | tf_op jit(solution)/shard_map/psum | solution.py:69
  828.2 0.7 fusion.51
  828.9 0.6 maximum_bitcast_fusion
  (45 shorter events, 0.1 us)
Async XLA Ops:
  8.0 21.9 %copy-start = (bf16[2048,128]{1,0:T(8,128)(2,1)S(1)}, bf16[2048,128]{1,0:T(8,128)(2,1)}, u32[]{:S(2)}) copy-start(bf16[2048,128]{1,0:T(8,128)(2,1)} %param.7) | copy-start | bytes 1572868
  9.5 29.1 %all-to-all-start.1 = ((bf16[64,8,128]{2,1,0:T(8,128)(2,1)}), bf16[64,8,128]{2,1,0:T(8,128)(2,1)S(1)}, u32[]{:S(2)}, u32[]{:S(2)}) async-start(bf16[64,8,128]{2,1,0:T(8,128)(2,1)} %stack.20), calls=%async_computation.1 | async-start | bytes 262144 | tf_op jit(solution)/shard_map/all_to_all | solution.py:25
  34.1 18.7 %copy-start.12 = (bf16[16,256,128]{2,1,0:T(8,128)(2,1)}, bf16[16,256,128]{2,1,0:T(8,128)(2,1)S(1)}, u32[]{:S(2)}) copy-start(bf16[16,256,128]{2,1,0:T(8,128)(2,1)S(1)} %gather_fusion.2) | copy-start | bytes 3145732
  39.3 24.9 %all-to-all-start.3 = ((bf16[64,8,128]{2,1,0:T(8,128)(2,1)}), bf16[64,8,128]{2,1,0:T(8,128)(2,1)S(1)}, u32[]{:S(2)}, u32[]{:S(2)}) async-start(bf16[64,8,128]{2,1,0:T(8,128)(2,1)} %stack.24), calls=%async_computation.3 | async-start | bytes 262144 | tf_op jit(solution)/shard_map/all_to_all | solution.py:25
  55.6 2.0 copy-start.13
  64.9 19.1 %all-to-all-start.2 = ((bf16[64,8,128]{2,1,0:T(8,128)(2,1)}), bf16[64,8,128]{2,1,0:T(8,128)(2,1)S(1)}, u32[]{:S(2)}, u32[]{:S(2)}) async-start(bf16[64,8,128]{2,1,0:T(8,128)(2,1)} %stack.22), calls=%async_computation.2 | async-start | bytes 262144 | tf_op jit(solution)/shard_map/all_to_all | solution.py:25
  73.5 3.5 copy-start.14
  77.1 2.1 copy-start.11
  84.7 22.2 %all-to-all-start = ((bf16[64,8,128]{2,1,0:T(8,128)(2,1)}), bf16[64,8,128]{2,1,0:T(8,128)(2,1)S(1)}, u32[]{:S(2)}, u32[]{:S(2)}) async-start(bf16[64,8,128]{2,1,0:T(8,128)(2,1)} %stack.18), calls=%async_computation | async-start | bytes 262144 | tf_op jit(solution)/shard_map/all_to_all | solution.py:25
  94.7 733.5 %all-reduce.3.cloned.1.call-start = ((), (), s32[]{:S(2)}) async-start(), calls=%async_computation.6 | async-start | bytes 2097152 | tf_op jit(solution)/shard_map/psum | solution.py:69
  96.6 3.5 copy-start.15
  100.2 2.1 copy-start.9
  108.6 3.5 copy-start.8
  112.0 1.4 copy-start.6
  115.4 3.4 copy-start.1
  118.1 3.5 copy-start.2
  120.8 3.7 copy-start.3
  124.5 3.1 copy-start.4
  127.5 702.0 %reduce-scatter.2.cloned.1.call-start = ((), (), s32[]{:S(2)}) async-start(), calls=%async_computation.5 | async-start | bytes 1310720 | tf_op jit(solution)/shard_map/reduce_scatter | solution.py:76
  127.6 2.0 copy-start.5
  129.6 2.0 copy-start.7
  129.6 2.0 copy-start.10
  131.6 1.2 copy-start.16
  135.1 693.1 %copy-start.17 = (f32[1,4,8,128]{3,2,1,0:T(8,128)S(1)}, f32[1,4,8,128]{3,2,1,0:T(8,128)}, u32[]{:S(2)}) copy-start(f32[1,4,8,128]{3,2,1,0:T(8,128)} %param.8) | copy-start | bytes 49156
Sparse Core Ops, SparseCore 0:
  127.7 700.4 all-reduce.2
Sparse Core Ops, SparseCore 1:
  136.3 21.4 reduce-scatter.1
